TPU v7x, 512 devices: a whole 4x4x16 slice. The times are simulated.
512 devices in a mesh: tm: 128 (over z, y, core), mod: 4 (over x).
Axes of the slice: x: 4, y: 4, z: 16, core: 2. Of those that a mesh axis runs over, the one named last changes fastest.
Arguments:
- filterbank: bfloat16 [16384, 128], P('tm'), may hold values from -6 to 6
- conv_weight: bfloat16 [384, 1280], replicated, may hold values from -0.3125 to 0.3125
- mlp_gain: float32 [1280], replicated, may hold values from 0.25 to 1.75
- up_weight: bfloat16 [1280, 5120], P('tm', 'mod'), may hold values from -0.15625 to 0.15625
- down_weight: bfloat16 [5120, 1280], P('mod', 'tm'), may hold values from -0.078125 to 0.078125
- post_gain: float32 [1280], replicated, may hold values from 0.25 to 1.75
- audio_weight: bfloat16 [1280, 1792], P(None, 'mod'), may hold values from -0.15625 to 0.15625
- patches: bfloat16 [32768, 1280], P('tm'), may hold values from -6 to 6
- vision_gain: float32 [1280], replicated, may hold values from 0.25 to 1.75
- vision_weight: bfloat16 [5120, 1792], P('tm', 'mod'), may hold values from -0.078125 to 0.078125
- retention: int32 [128, 64], P('tm'), may hold values from 0 to 63, each once within a row
- kept_count: int32 [128], P('tm'), may hold values from 1 to 64, 4096 in all
Outputs:
- sequence: bfloat16 [128, 96, 1792], P('tm', None, 'mod')
Inputs may be any that keep to these rules, and one draw needn't show every extreme that they name: `retention`: each row lists every merged token of its frame once. `kept_count`: the counts sum to 4096.
All inputs are finite; a program needn't handle non-finite values. No bound on the sum of `kept_count` on one device may be relied on, other than what follows from the above.
Results may differ from a plain program's by a relative error of at most 0.01.
Values may be sent and summed in bfloat16 or wider, within the bound.
No kernel may reach another device: no remote copies, remote signals or barrier semaphores. Data moves between devices by JAX's collectives and lax.ppermute only.
A program may use at most 64 MiB of HBM per device.

v0:
```python
import jax
import jax.numpy as jnp
from jax import lax
from jax.sharding import PartitionSpec as P

MRG_FRAME = 64
AUD_TOK = 64
SEQ_DEV = 96


def carried_in(value, axis, join, neutral):
    count, mine = (lax.axis_size(axis), lax.axis_index(axis))
    pieces = lax.all_gather(value, axis)
    running = jnp.full_like(value, 0) + jnp.asarray(neutral, value.dtype)

    def hop(position, running):
        longer = join(running, pieces[position])
        return jnp.where(position < mine, longer, running)

    return lax.fori_loop(0, count - 1, hop, running)


def padded(shard, sides, width):
    for axis, dim in sides:
        peers, length = (lax.axis_size(axis), shard.shape[dim])
        up = [(i, (i + 1) % peers) for i in range(peers - 1)]
        down = [(j, i) for i, j in up]
        last = lax.slice_in_dim(shard, length - width, length, axis=dim)
        first = lax.slice_in_dim(shard, 0, width, axis=dim)
        before = lax.ppermute(last, axis, up)
        after = lax.ppermute(first, axis, down)
        shard = jnp.concatenate([before, shard, after], axis=dim)
    return shard


def layer_norm(values, scale_gain):
    average = jnp.mean(values, axis=-1, keepdims=True)
    centred = values - average
    variance = jnp.mean(centred * centred, axis=-1, keepdims=True)
    return centred * lax.rsqrt(variance + 1e-05) * scale_gain


def rms_norm(values, scale_gain):
    square_mean = jnp.mean(values * values, axis=-1, keepdims=True)
    return values * lax.rsqrt(square_mean + 1e-06) * scale_gain


def pool_pairs(values):
    return values.reshape(-1, 2, values.shape[-1]).mean(axis=1)


def add_counts(earlier, later):
    return earlier + later


def on_device(
    filterbank,
    conv_weight,
    mlp_gain,
    up_weight,
    down_weight,
    post_gain,
    audio_weight,
    patches,
    vision_gain,
    vision_weight,
    retention,
    kept_count,
):
    placed = kept_count + AUD_TOK
    starts = carried_in(placed, "tm", add_counts, jnp.zeros((1,), jnp.int32))
    framed = padded(filterbank, (("tm", 0),), 1)
    unfolded = jnp.concatenate([framed[:-2], framed[1:-1], framed[2:]], axis=1)
    stem = jax.nn.gelu(
        jnp.dot(unfolded, conv_weight, preferred_element_type=jnp.float32), approximate=False
    ).astype(jnp.bfloat16)
    residual = stem.astype(jnp.float32)
    hidden = layer_norm(residual, mlp_gain).astype(jnp.bfloat16)
    up_share = lax.all_gather(up_weight, "tm", axis=0, tiled=True)
    pre_act = jnp.dot(hidden, up_share, preferred_element_type=jnp.float32)
    activated = jax.nn.gelu(pre_act, approximate=False).astype(jnp.bfloat16)
    down_share = lax.all_gather(down_weight, "tm", axis=1, tiled=True)
    partial_value = jnp.dot(activated, down_share, preferred_element_type=jnp.float32)
    summed = lax.psum(partial_value.astype(jnp.bfloat16), "mod").astype(jnp.float32)
    pooled = pool_pairs(residual + summed)
    normed = layer_norm(pooled, post_gain).astype(jnp.bfloat16)
    audio_tokens = jnp.dot(normed, audio_weight, preferred_element_type=jnp.float32).astype(
        jnp.bfloat16
    )
    patch_normed = rms_norm(patches.astype(jnp.float32), vision_gain).astype(jnp.bfloat16)
    merged = patch_normed.reshape(-1, 4 * patch_normed.shape[1])
    vision_share = lax.all_gather(vision_weight, "tm", axis=0, tiled=True)
    visual_tokens = jnp.dot(merged, vision_share, preferred_element_type=jnp.float32).astype(
        jnp.bfloat16
    )
    peer_count = lax.axis_size("tm")
    per_peer = (AUD_TOK + MRG_FRAME + peer_count - 1) // peer_count
    kept_here = kept_count[0]
    first_slot = starts[0]
    all_tokens = jnp.concatenate([visual_tokens, audio_tokens], axis=0)
    peer_ids = jnp.arange(peer_count, dtype=jnp.int32)[:, None]
    round_ids = jnp.arange(per_peer, dtype=jnp.int32)[None, :]
    local_index = round_ids * peer_count + (peer_ids - first_slot) % peer_count
    valid_rows = local_index < kept_here + AUD_TOK
    kept_index = jnp.take(retention[0], jnp.minimum(local_index, MRG_FRAME - 1), axis=0)
    source_index = jnp.where(
        local_index < kept_here, kept_index, MRG_FRAME + local_index - kept_here
    )
    source_index = jnp.where(valid_rows, source_index, 0).astype(jnp.int32)
    send_rows = jnp.take(all_tokens, source_index.reshape(-1), axis=0).reshape(
        peer_count, per_peer, all_tokens.shape[1]
    )
    send_slots = jnp.where(valid_rows, (first_slot + local_index) // peer_count, SEQ_DEV).astype(
        jnp.int32
    )
    recv_rows, recv_slots = (
        lax.all_to_all(send_rows, "tm", split_axis=0, concat_axis=0, tiled=True),
        lax.all_to_all(send_slots, "tm", split_axis=0, concat_axis=0, tiled=True),
    )
    sequence = jnp.zeros((SEQ_DEV, all_tokens.shape[1]), jnp.bfloat16)
    sequence = sequence.at[recv_slots.reshape(-1)].set(
        recv_rows.reshape(-1, all_tokens.shape[1]), mode="drop"
    )
    return sequence[None]


def solution(mesh):
    return jax.shard_map(
        on_device,
        mesh=mesh,
        in_specs=(
            P("tm", None),
            P(),
            P(),
            P("tm", "mod"),
            P("mod", "tm"),
            P(),
            P(None, "mod"),
            P("tm", None),
            P(),
            P("tm", "mod"),
            P("tm", None),
            P("tm"),
        ),
        out_specs=P("tm", None, "mod"),
        check_vma=False,
    )
```

profile of v0, /device:TPU:33, one launch (start us, length us, event | category | flops | bytes accessed | tf_op | source)
XLA Modules:
  0.0 566.4 jit_solution(12969941539579024190)
XLA Ops:
  8.8 3.8 collective-permute-start
  12.5 1.9 collective-permute-start.1
  14.5 2.9 collective-permute-done.1
  17.4 3.0 convert_reduce_fusion
  20.6 137.2 %all-gather.9.cloned.1.call-done = bf16[128,10,1280]{2,1,0:T(8,128)(2,1)} async-done(((bf16[1,10,1280]{2,1,0:T(8,128)(2,1)}), bf16[128,10,1280]{2,1,0:T(8,128)(2,1)}) %all-gather.9.cloned.1.call-update) | async-done | bytes 3276816 | tf_op jit(solution)/shard_map/all_gather | solution.py:79
  157.8 7.0 %reshape.396 = bf16[1280,1280]{1,0:T(8,128)(2,1)} reshape(bf16[128,10,1280]{2,1,0:T(8,128)(2,1)} %all-gather.9.cloned.1.call-done) | data formatting | bytes 6553600
  164.9 134.5 %all-gather.11.cloned.1.call-done = bf16[128,10,1280]{2,1,0:T(8,128)(2,1)} async-done(((bf16[1,10,1280]{2,1,0:T(8,128)(2,1)}), bf16[128,10,1280]{2,1,0:T(8,128)(2,1)}) %all-gather.11.cloned.1.call-update) | async-done | bytes 3276816 | tf_op jit(solution)/shard_map/all_gather | solution.py:82
  299.4 7.0 %reshape.398 = bf16[1280,1280]{1,0:T(8,128)(2,1)} reshape(bf16[128,10,1280]{2,1,0:T(8,128)(2,1)} %all-gather.11.cloned.1.call-done) | data formatting | bytes 6553600
  306.5 6.5 %convolution_convert_fusion = bf16[128,1280]{1,0:T(8,128)(2,1)} fusion(bf16[1280,1280]{1,0:T(8,128)(2,1)} %reshape.398, bf16[1280,1280]{1,0:T(8,128)(2,1)} %reshape.396, bf16[128,1280]{1,0:T(8,128)(2,1)S(1)} %get-tuple-element.96, f32[1280]{0:T(1024)S(1)} %copy-done.5, f32[128]{0:T(128)S(1)} %add_rsqrt_fusion.2, f32[128]{0:T(128)S(1)} %broadcast_multiply_fusion.1), kind=kOutput, calls=%fused_computation.4 | convolution fusion | flops 850493440 | bytes 7215104 | tf_op jit(solution)/shard_map/dot_general | solution.py:83
  314.2 1.3 dynamic-slice
  316.2 19.5 %all-reduce = s32[128]{0:T(128)S(1)} all-reduce(s32[128]{0:T(128)S(1)} %add_dynamic-update-slice_fusion), channel_id=2, replica_groups=mesh['tm'=128,'mod'=4] {'tm'}, use_global_device_ids=true, to_apply=%add | all-reduce | flops 128 | bytes 1024
  335.8 157.1 %while.13 = (s32[]{:T(128)}, s32[1]{0:T(128)}, s32[]{:T(128)}, s32[128,1]{0,1:T(1,128)S(1)}, s32[]{:T(128)}) while((s32[]{:T(128)}, s32[1]{0:T(128)}, s32[]{:T(128)}, s32[128,1]{0,1:T(1,128)S(1)}, s32[]{:T(128)}) %tuple.41), condition=%wide.region_1.2_spmd, body=%wide.region_0.1_spmd.sunk | while | flops 5 | bytes 107 | solution.py:20
  492.9 1.2 compare_select_fusion.3
  494.1 16.5 %all-to-all-start = ((s32[128,1,1]{2,1,0:T(1,128)}), s32[128,1,1]{2,1,0:T(1,128)S(1)}, u32[]{:S(2)}, u32[]{:S(2)}) async-start(s32[128,1,1]{2,1,0:T(1,128)} %compare_select_fusion.3), calls=%async_computation | async-start | bytes 131072 | tf_op jit(solution)/shard_map/all_to_all | solution.py:118
  511.4 2.5 fusion.89
  513.9 1.2 gather_fusion
  515.2 1.0 convert_add_fusion
  516.7 0.8 reduce_sum.57
  518.3 3.5 convolution_convert_fusion.2
  521.9 0.8 gather_fusion.1
  524.9 16.1 %all-to-all-start.1 = ((bf16[128,2,224]{2,1,0:T(2,128)(2,1)}), bf16[128,2,224]{2,1,0:T(2,128)(2,1)S(1)}, u32[]{:S(2)}, u32[]{:S(2)}) async-start(bf16[128,2,224]{2,1,0:T(2,128)(2,1)} %reshape.405), calls=%async_computation.1 | async-start | bytes 262144 | tf_op jit(solution)/shard_map/all_to_all | solution.py:117
  541.0 2.4 reduce
  543.4 14.7 %all-to-all-done.1 = bf16[128,2,224]{2,1,0:T(2,128)(2,1)S(1)} async-done(((bf16[128,2,224]{2,1,0:T(2,128)(2,1)}), bf16[128,2,224]{2,1,0:T(2,128)(2,1)S(1)}, u32[]{:S(2)}, u32[]{:S(2)}) %all-to-all-start.1) | async-done | bytes 114720 | tf_op jit(solution)/shard_map/all_to_all | solution.py:117
  558.3 1.6 scatter_custom_fusion
  (178 shorter events, 83.6 us)
Async XLA Ops:
  6.5 511.3 %copy-start = (bf16[1280,448]{0,1:T(8,128)(2,1)S(1)}, bf16[1280,448]{0,1:T(8,128)(2,1)}, u32[]{:S(2)}) copy-start(bf16[1280,448]{0,1:T(8,128)(2,1)} %param.20) | copy-start | bytes 3440644
  6.5 151.3 %all-gather.9.cloned.1.call-start = ((), (), s32[]{:S(2)}) async-start(), calls=%async_computation.4 | async-start | bytes 5283840 | tf_op jit(solution)/shard_map/all_gather | solution.py:79
  7.3 292.1 %all-gather.11.cloned.1.call-start = ((), (), s32[]{:S(2)}) async-start(), calls=%async_computation.5 | async-start | bytes 5283840 | tf_op jit(solution)/shard_map/all_gather | solution.py:82
  8.0 507.2 %all-reduce.3.cloned.1.call-start = ((), (), s32[]{:S(2)}) async-start(), calls=%async_computation.3 | async-start | bytes 655360 | tf_op jit(solution)/shard_map/psum | solution.py:84
  8.8 5.7 %collective-permute-start = (bf16[1,128]{1,0:T(2,128)(2,1)S(1)}, bf16[1,128]{1,0:T(2,128)(2,1)S(1)}, u32[]{:S(2)}, u32[]{:S(2)}) collective-permute-start(bf16[1,128]{1,0:T(2,128)(2,1)S(1)} %get-tuple-element.93), channel_id=1, source_target_pairs={{0,4},{4,8},{8,12},{12,16},{16,20},{20,24},{24,28},{28,32},{32,36}... | collective-permute-start | bytes 776 | tf_op jit(solution)/shard_map/ppermute | solution.py:30
  12.5 4.9 collective-permute-start.1
  164.9 141.6 %copy-start.5 = (f32[1280]{0:T(1024)S(1)}, f32[1280]{0:T(1024)}, u32[]{:S(2)}) copy-start(f32[1280]{0:T(1024)} %param.16) | copy-start | bytes 15364
  306.5 204.1 %copy-start.2 = (bf16[256,1280]{1,0:T(8,128)(2,1)S(1)}, bf16[256,1280]{1,0:T(8,128)(2,1)}, u32[]{:S(2)}) copy-start(bf16[256,1280]{1,0:T(8,128)(2,1)} %param.21) | copy-start | bytes 1966084
  306.5 204.3 %copy-start.3 = (f32[1280]{0:T(1024)S(1)}, f32[1280]{0:T(1024)}, u32[]{:S(2)}) copy-start(f32[1280]{0:T(1024)} %param.22) | copy-start | bytes 15364
  313.0 200.9 %copy-start.1 = (s32[1,64]{1,0:T(1,128)S(1)}, s32[1,64]{1,0:T(1,128)}, u32[]{:S(2)}) copy-start(s32[1,64]{1,0:T(1,128)} %param.24) | copy-start | bytes 772
  313.0 205.3 %all-gather.7.cloned.1.call-start = ((), (), s32[]{:S(2)}) async-start(), calls=%async_computation.2 | async-start | bytes 5283840 | tf_op jit(solution)/shard_map/all_gather | solution.py:92
  494.1 30.8 %all-to-all-start = ((s32[128,1,1]{2,1,0:T(1,128)}), s32[128,1,1]{2,1,0:T(1,128)S(1)}, u32[]{:S(2)}, u32[]{:S(2)}) async-start(s32[128,1,1]{2,1,0:T(1,128)} %compare_select_fusion.3), calls=%async_computation | async-start | bytes 131072 | tf_op jit(solution)/shard_map/all_to_all | solution.py:118
  511.0 6.8 %copy-start.4 = (f32[1280]{0:T(1024)S(1)}, f32[1280]{0:T(1024)}, u32[]{:S(2)}) copy-start(f32[1280]{0:T(1024)} %param.19) | copy-start | bytes 15364
  524.9 33.2 %all-to-all-start.1 = ((bf16[128,2,224]{2,1,0:T(2,128)(2,1)}), bf16[128,2,224]{2,1,0:T(2,128)(2,1)S(1)}, u32[]{:S(2)}, u32[]{:S(2)}) async-start(bf16[128,2,224]{2,1,0:T(2,128)(2,1)} %reshape.405), calls=%async_computation.1 | async-start | bytes 262144 | tf_op jit(solution)/shard_map/all_to_all | solution.py:117
Sparse Core Ops, SparseCore 0:
  10.5 147.3 all-gather.8
  161.0 138.3 all-gather.10
  313.1 50.4 all-reduce.2
  366.6 146.1 all-gather.6
where the time goes:
time: 574 us; the launch traced here: 566 us
  waiting for transfers between devices  291 us (51%)
  local copies, waits for them, and re-layouts  97.5 us (17%)
  loops' own time  81.7 us (14%)
  starting transfers between devices  38.4 us (7%)
  blocking collectives  19.5 us (3%)
  between operations  14 us (2%)
  matrix products  13.5 us (2%)
  other arithmetic  10.4 us (2%)
    all_gather x1, waiting for transfers between devices, on_device(): up_share = lax.all_gather(up_weight, 'tm', axis=0, tiled=True)  137 us
    all_gather x1, waiting for transfers between devices, on_device(): down_share = lax.all_gather(down_weight, 'tm', axis=1, tiled=True)  135 us
    another operation x1, loops' own time, carried_in(): return lax.fori_loop(0, count - 1, hop, running)  81.7 us
    dynamic_slice x127, local copies, waits for them, and re-layouts, hop(): longer = join(running, pieces[position])  75.4 us
    unnamed x1, blocking collectives  19.5 us
    all_to_all x1, starting transfers between devices, on_device(): lax.all_to_all(send_slots, 'tm', split_axis=0, concat_axis=0, tiled=True)  16.5 us
    unnamed x18, local copies, waits for them, and re-layouts  16.3 us
    all_to_all x1, starting transfers between devices, on_device(): lax.all_to_all(send_rows, 'tm', split_axis=0, concat_axis=0, tiled=True)  16.1 us
  transfers between devices with their start and end apart: 8, of which 4 were waited for; matrix products, arithmetic and copies ran while one was open for 19% of the time, Pallas kernels for 0%

commit v1 on v0

--- a/solution.py
+++ b/solution.py
@@ -76,7 +76,15 @@
     ).astype(jnp.bfloat16)
     residual = stem.astype(jnp.float32)
     hidden = layer_norm(residual, mlp_gain).astype(jnp.bfloat16)
-    up_share = lax.all_gather(up_weight, "tm", axis=0, tiled=True)
+    up_share = jnp.concatenate(
+        lax.all_to_all(
+            jnp.stack([up_weight for _ in range(lax.axis_size("tm"))]),
+            axis_name="tm",
+            split_axis=0,
+            concat_axis=0,
+        ),
+        axis=0,
+    )
     pre_act = jnp.dot(hidden, up_share, preferred_element_type=jnp.float32)
     activated = jax.nn.gelu(pre_act, approximate=False).astype(jnp.bfloat16)
     down_share = lax.all_gather(down_weight, "tm", axis=1, tiled=True)

time: 574 us -> 616 us (1.073)
  blocking collectives: 19.5 us -> 247 us
  waiting for transfers between devices: 291 us -> 68.9 us
  starting transfers between devices: 38.4 us -> 63.2 us
  local copies, waits for them, and re-layouts: 97.5 us -> 108 us
  loops' own time: 81.7 us -> 88.9 us
    unnamed x1, blocking collectives: 19.5 us -> 247 us
    all_gather x1 -> x0, waiting for transfers between devices: 137 us -> none  [on_device(): up_share = lax.all_gather(up_weight, 'tm', axis=0, tiled=True)]
    all_gather x1, waiting for transfers between devices: 135 us -> 0.02 us  [on_device(): down_share = lax.all_gather(down_weight, 'tm', axis=1, tiled=True)]
    psum x1, waiting for transfers between devices: 0.02 us -> 52.7 us  [on_device(): lax.psum(partial_value.astype(jnp.bfloat16), 'mod').astype(jnp.float32)]
    all_to_all x0 -> x1, starting transfers between devices: none -> 20 us  [on_device(): lax.all_to_all(jnp.stack([up_weight for _ in range(lax.axis_size('tm'))])...]
    dynamic_slice x127, local copies, waits for them, and re-layouts: 75.4 us -> 83.4 us  [hop(): longer = join(running, pieces[position])]
    another operation x1, loops' own time: 81.7 us -> 88.9 us  [carried_in(): return lax.fori_loop(0, count - 1, hop, running)]
    reshape x0 -> x1, local copies, waits for them, and re-layouts: none -> 7.02 us  [on_device(): jnp.concatenate(lax.all_to_all(jnp.stack([up_weight for _ in range(lax.ax...]
  transfers between devices with their start and end apart: 8 -> 8, of which waited for: 4 -> 2; matrix products, arithmetic and copies ran while one was open for 19% -> 21% of each run, Pallas kernels for 0% -> 0%
where the time goes in v1:
time: 616 us; the launch traced here: 614 us
  blocking collectives  247 us (40%)
  local copies, waits for them, and re-layouts  108 us (18%)
  loops' own time  88.9 us (14%)
  waiting for transfers between devices  68.9 us (11%)
  starting transfers between devices  63.2 us (10%)
  between operations  14 us (2%)
  matrix products  13.3 us (2%)
  other arithmetic  10.5 us (2%)
    unnamed x1, blocking collectives  247 us
    another operation x1, loops' own time, carried_in(): return lax.fori_loop(0, count - 1, hop, running)  88.9 us
    dynamic_slice x127, local copies, waits for them, and re-layouts, hop(): longer = join(running, pieces[position])  83.4 us
    psum x1, waiting for transfers between devices, on_device(): lax.psum(partial_value.astype(jnp.bfloat16), 'mod').astype(jnp.float32)  52.7 us
    all_to_all x1, starting transfers between devices, on_device(): lax.all_to_all(jnp.stack([up_weight for _ in range(lax.axis_size('tm'))])...  20 us
    all_to_all x1, starting transfers between devices, on_device(): lax.all_to_all(send_rows, 'tm', split_axis=0, concat_axis=0, tiled=True)  18.9 us
    all_to_all x1, starting transfers between devices, on_device(): lax.all_to_all(send_slots, 'tm', split_axis=0, concat_axis=0, tiled=True)  18.8 us
    all_to_all x1, waiting for transfers between devices, on_device(): lax.all_to_all(send_rows, 'tm', split_axis=0, concat_axis=0, tiled=True)  14.7 us
  transfers between devices with their start and end apart: 8, of which 2 were waited for; matrix products, arithmetic and copies ran while one was open for 21% of the time, Pallas kernels for 0%

profile of v1, /device:TPU:33, one launch (start us, length us, event | category | flops | bytes accessed | tf_op | source)
XLA Modules:
  0.0 614.2 jit_solution(17638119141574757490)
XLA Ops:
  7.3 3.4 stack.2
  10.6 20.0 %all-to-all-start.1 = ((bf16[128,10,1280]{2,1,0:T(8,128)(2,1)}), bf16[128,10,1280]{2,1,0:T(8,128)(2,1)}, u32[]{:S(2)}, u32[]{:S(2)}) async-start(bf16[128,10,1280]{2,1,0:T(8,128)(2,1)} %stack.2), calls=%async_computation.1 | async-start | bytes 10485760 | tf_op jit(solution)/shard_map/all_to_all | solution.py:80
  31.4 3.4 collective-permute-start
  34.8 1.9 collective-permute-start.1
  37.4 1.3 dynamic-slice
  39.5 247.2 %all-reduce = s32[128]{0:T(128)S(1)} all-reduce(s32[128]{0:T(128)S(1)} %add_dynamic-update-slice_fusion), channel_id=2, replica_groups=mesh['tm'=128,'mod'=4] {'tm'}, use_global_device_ids=true, to_apply=%add | all-reduce | flops 128 | bytes 1024
  286.7 172.2 %while.13 = (s32[]{:T(128)}, s32[1]{0:T(128)}, s32[]{:T(128)}, s32[128,1]{0,1:T(1,128)S(1)}, s32[]{:T(128)}) while((s32[]{:T(128)}, s32[1]{0:T(128)}, s32[]{:T(128)}, s32[128,1]{0,1:T(1,128)S(1)}, s32[]{:T(128)}) %tuple.39), condition=%wide.region_1.2_spmd, body=%wide.region_0.1_spmd.sunk | while | flops 5 | bytes 107 | solution.py:20
  458.9 2.5 fusion.89
  461.4 1.2 gather_fusion
  462.7 1.2 compare_select_fusion.3
  464.8 2.9 convert_reduce_fusion
  468.0 7.0 %reshape.402 = bf16[1280,1280]{1,0:T(8,128)(2,1)} reshape(bf16[128,10,1280]{2,1,0:T(8,128)(2,1)} %all-gather.7.cloned.1.call-done) | data formatting | bytes 6553600
  475.0 18.8 %all-to-all-start = ((s32[128,1,1]{2,1,0:T(1,128)}), s32[128,1,1]{2,1,0:T(1,128)S(1)}, u32[]{:S(2)}, u32[]{:S(2)}) async-start(s32[128,1,1]{2,1,0:T(1,128)} %compare_select_fusion.3), calls=%async_computation | async-start | bytes 131072 | tf_op jit(solution)/shard_map/all_to_all | solution.py:126
  494.0 7.0 %reshape.369 = bf16[1280,1280]{1,0:T(8,128)(2,1)} reshape(bf16[128,10,1280]{2,1,0:T(8,128)(2,1)} %all-to-all-done.1) | data formatting | bytes 6553600 | tf_op jit(solution)/shard_map/reshape | solution.py:79
  501.0 6.4 %convolution_convert_fusion = bf16[128,1280]{1,0:T(8,128)(2,1)} fusion(bf16[1280,1280]{1,0:T(8,128)(2,1)} %reshape.402, bf16[1280,1280]{1,0:T(8,128)(2,1)} %reshape.369, bf16[128,1280]{1,0:T(8,128)(2,1)S(1)} %get-tuple-element.96, f32[1280]{0:T(1024)S(1)} %copy-done.6, f32[128]{0:T(128)S(1)} %add_rsqrt_fusion.2, f32[128]{0:T(128)S(1)} %broadcast_multiply_fusion.1), kind=kOutput, calls=%fused_computation.4 | convolution fusion | flops 850493440 | bytes 7215104 | tf_op jit(solution)/shard_map/dot_general | solution.py:91
  507.5 3.5 convolution_convert_fusion.2
  511.0 52.7 %all-reduce.3.cloned.1.call-done = bf16[128,1280]{1,0:T(8,128)(2,1)} async-done(((bf16[128,1280]{1,0:T(8,128)(2,1)}), bf16[128,1280]{1,0:T(8,128)(2,1)}) %all-reduce.3.cloned.1.call-update) | async-done | bytes 327696 | tf_op jit(solution)/shard_map/psum | solution.py:92
  563.7 1.0 convert_add_fusion
  565.2 0.8 reduce_sum.57
  566.8 0.8 gather_fusion.1
  569.8 18.9 %all-to-all-start.2 = ((bf16[128,2,224]{2,1,0:T(2,128)(2,1)}), bf16[128,2,224]{2,1,0:T(2,128)(2,1)S(1)}, u32[]{:S(2)}, u32[]{:S(2)}) async-start(bf16[128,2,224]{2,1,0:T(2,128)(2,1)} %reshape.409), calls=%async_computation.2 | async-start | bytes 262144 | tf_op jit(solution)/shard_map/all_to_all | solution.py:125
  588.7 2.4 reduce
  591.1 14.7 %all-to-all-done.2 = bf16[128,2,224]{2,1,0:T(2,128)(2,1)S(1)} async-done(((bf16[128,2,224]{2,1,0:T(2,128)(2,1)}), bf16[128,2,224]{2,1,0:T(2,128)(2,1)S(1)}, u32[]{:S(2)}, u32[]{:S(2)}) %all-to-all-start.2) | async-done | bytes 114720 | tf_op jit(solution)/shard_map/all_to_all | solution.py:125
  606.0 1.6 scatter_custom_fusion
  (180 shorter events, 90.6 us)
Async XLA Ops:
  6.5 559.7 %copy-start = (bf16[1280,448]{0,1:T(8,128)(2,1)S(1)}, bf16[1280,448]{0,1:T(8,128)(2,1)}, u32[]{:S(2)}) copy-start(bf16[1280,448]{0,1:T(8,128)(2,1)} %param.20) | copy-start | bytes 3440644
  6.5 461.4 %all-gather.7.cloned.1.call-start = ((), (), s32[]{:S(2)}) async-start(), calls=%async_computation.5 | async-start | bytes 5283840 | tf_op jit(solution)/shard_map/all_gather | solution.py:90
  10.6 20.8 %copy-start.5 = (bf16[128,128]{1,0:T(8,128)(2,1)S(1)}, bf16[128,128]{1,0:T(8,128)(2,1)}, u32[]{:S(2)}) copy-start(bf16[128,128]{1,0:T(8,128)(2,1)} %param.14) | copy-start | bytes 98308
  10.6 450.8 %copy-start.1 = (s32[1,64]{1,0:T(1,128)S(1)}, s32[1,64]{1,0:T(1,128)}, u32[]{:S(2)}) copy-start(s32[1,64]{1,0:T(1,128)} %param.24) | copy-start | bytes 772
  10.6 453.2 %copy-start.2 = (bf16[256,1280]{1,0:T(8,128)(2,1)S(1)}, bf16[256,1280]{1,0:T(8,128)(2,1)}, u32[]{:S(2)}) copy-start(bf16[256,1280]{1,0:T(8,128)(2,1)} %param.21) | copy-start | bytes 1966084
  10.6 453.5 %copy-start.3 = (f32[1280]{0:T(1024)S(1)}, f32[1280]{0:T(1024)}, u32[]{:S(2)}) copy-start(f32[1280]{0:T(1024)} %param.22) | copy-start | bytes 15364
  10.6 464.4 %all-to-all-start.1 = ((bf16[128,10,1280]{2,1,0:T(8,128)(2,1)}), bf16[128,10,1280]{2,1,0:T(8,128)(2,1)}, u32[]{:S(2)}, u32[]{:S(2)}) async-start(bf16[128,10,1280]{2,1,0:T(8,128)(2,1)} %stack.2), calls=%async_computation.1 | async-start | bytes 10485760 | tf_op jit(solution)/shard_map/all_to_all | solution.py:80
  30.6 476.9 %all-gather.5.cloned.1.call-start = ((), (), s32[]{:S(2)}) async-start(), calls=%async_computation.3 | async-start | bytes 5283840 | tf_op jit(solution)/shard_map/all_gather | solution.py:100
  31.4 433.3 %collective-permute-start = (bf16[1,128]{1,0:T(2,128)(2,1)S(1)}, bf16[1,128]{1,0:T(2,128)(2,1)S(1)}, u32[]{:S(2)}, u32[]{:S(2)}) collective-permute-start(bf16[1,128]{1,0:T(2,128)(2,1)S(1)} %get-tuple-element.93), channel_id=1, source_target_pairs={{0,4},{4,8},{8,12},{12,16},{16,20},{20,24},{24,28},{28,32},{32,36}... | collective-permute-start | bytes 776 | tf_op jit(solution)/shard_map/ppermute | solution.py:30
  34.8 430.0 %collective-permute-start.1 = (bf16[1,128]{1,0:T(2,128)(2,1)S(1)}, bf16[1,128]{1,0:T(2,128)(2,1)S(1)}, u32[]{:S(2)}, u32[]{:S(2)}) collective-permute-start(bf16[1,128]{1,0:T(2,128)(2,1)S(1)} %get-tuple-element.94), channel_id=1, source_target_pairs={{4,0},{8,4},{12,8},{16,12},{20,16},{24,20},{28,24},{32,28},{36,32}... | collective-permute-start | bytes 776 | tf_op jit(solution)/shard_map/ppermute | solution.py:31
  475.0 94.8 %all-to-all-start = ((s32[128,1,1]{2,1,0:T(1,128)}), s32[128,1,1]{2,1,0:T(1,128)S(1)}, u32[]{:S(2)}, u32[]{:S(2)}) async-start(s32[128,1,1]{2,1,0:T(1,128)} %compare_select_fusion.3), calls=%async_computation | async-start | bytes 131072 | tf_op jit(solution)/shard_map/all_to_all | solution.py:126
  493.8 7.3 %copy-start.6 = (f32[1280]{0:T(1024)S(1)}, f32[1280]{0:T(1024)}, u32[]{:S(2)}) copy-start(f32[1280]{0:T(1024)} %param.16) | copy-start | bytes 15364
  493.8 69.9 %all-reduce.3.cloned.1.call-start = ((), (), s32[]{:S(2)}) async-start(), calls=%async_computation.4 | async-start | bytes 655360 | tf_op jit(solution)/shard_map/psum | solution.py:92
  511.0 55.3 %copy-start.4 = (f32[1280]{0:T(1024)S(1)}, f32[1280]{0:T(1024)}, u32[]{:S(2)}) copy-start(f32[1280]{0:T(1024)} %param.19) | copy-start | bytes 15364
  569.8 36.0 %all-to-all-start.2 = ((bf16[128,2,224]{2,1,0:T(2,128)(2,1)}), bf16[128,2,224]{2,1,0:T(2,128)(2,1)S(1)}, u32[]{:S(2)}, u32[]{:S(2)}) async-start(bf16[128,2,224]{2,1,0:T(2,128)(2,1)} %reshape.409), calls=%async_computation.2 | async-start | bytes 262144 | tf_op jit(solution)/shard_map/all_to_all | solution.py:125
Sparse Core Ops, SparseCore 0:
  10.5 185.3 all-gather.6
  199.0 160.9 all-gather.4
  507.6 56.0 all-reduce.2
